TPU v7x, 32 devices: a whole 2x2x4 slice. The times are simulated.
32 devices in a mesh: frame: 8 (over y, x, core), query: 4 (over z).
Axes of the slice: x: 2, y: 2, z: 4, core: 2. Of those that a mesh axis runs over, the one named last changes fastest.
Arguments:
- features: bfloat16 [8, 4096, 256], P('frame'), may hold values from -4.375 to 4.375
- kernel: float32 [3, 3], replicated, may hold values from 0.2 to 1
- cotangent: float32 [2, 8, 4096], P(None, 'frame', 'query'), may hold values from -6 to 6
- query_frame: int32 [4096], P('query'), may hold values from 0 to 7
- query_pixel: int32 [4096], P('query'), may hold values from 0 to 4095
Outputs:
- query_grad: float32 [4096, 256], P('query')
- feature_grad: float32 [8, 4096, 256], P('frame', 'query')
All inputs are finite; a program needn't handle non-finite values.
Results may differ from a plain program's by a relative error of at most 0.0029.
Values may be sent and summed in bfloat16 or wider, within the bound.
No kernel may reach another device: no remote copies, remote signals or barrier semaphores. Data moves between devices by JAX's collectives and lax.ppermute only.
A program may use at most 128 MiB of HBM per device.

v0:
```python
import jax
import jax.numpy as jnp
from jax import lax
from jax.sharding import PartitionSpec as P

W = 64


def shifted(values, offset, margin, length):
    padded = jnp.pad(values, ((0, 0), (margin, margin)))
    return lax.slice_in_dim(padded, margin + offset, margin + offset + length, axis=1)


def shards(features, kernel, cotangent, query_frame, query_pixel):
    t_dev, pixels, chan = features.shape
    height = pixels // W
    margin = W + 1
    frame_base = lax.axis_index("frame") * t_dev
    local_frame = query_frame - frame_base
    owned = (local_frame >= 0) & (local_frame < t_dev)
    flat_rows = jnp.clip(local_frame, 0, t_dev - 1) * pixels + query_pixel
    flat_maps = features.reshape(t_dev * pixels, chan)
    picked = jnp.where(owned[:, None], flat_maps[flat_rows], 0).astype(jnp.float32)
    qfeat = lax.psum(picked.astype(jnp.bfloat16), "frame")
    where_pix = lax.iota(jnp.int32, pixels)
    column = where_pix % W
    row_pos = (where_pix // W).astype(jnp.float32) - (height - 1) / 2.0
    col_pos = column.astype(jnp.float32) - (W - 1) / 2.0
    col_masks = {
        -1: (column >= 1)[None, :],
        0: (column >= 0)[None, :],
        1: (column <= W - 2)[None, :],
    }
    frame_map = features[0]
    cost = lax.dot_general(
        qfeat, frame_map, (((1,), (1,)), ((), ())), preferred_element_type=jnp.float32
    )
    logits = jnp.zeros_like(cost)
    for a in (-1, 0, 1):
        for b in (-1, 0, 1):
            moved = shifted(cost, a * W + b, margin, pixels)
            logits = logits + kernel[a + 1, b + 1] * jnp.where(col_masks[b], moved, 0.0)
    top = jnp.max(logits, axis=1, keepdims=True)
    expo = jnp.exp(logits - top)
    prob = expo / jnp.sum(expo, axis=1, keepdims=True)
    pull = cotangent[0, 0][:, None] * row_pos[None, :] + cotangent[1, 0][:, None] * col_pos[None, :]
    mean_pull = jnp.sum(prob * pull, axis=1, keepdims=True)
    dlogit = prob * (pull - mean_pull)
    dcost = jnp.zeros_like(dlogit)
    for a in (-1, 0, 1):
        for b in (-1, 0, 1):
            masked = jnp.where(col_masks[b], dlogit, 0.0)
            dcost = dcost + kernel[a + 1, b + 1] * shifted(masked, -(a * W + b), margin, pixels)
    dcost = dcost.astype(jnp.bfloat16)
    query_part = jnp.dot(dcost, frame_map, preferred_element_type=jnp.float32)
    frame_terms = [
        lax.dot_general(dcost, qfeat, (((0,), (0,)), ((), ())), preferred_element_type=jnp.float32)
    ]
    feature_term = jnp.stack(frame_terms)
    query_grad = lax.psum(query_part, "frame")
    placed = jnp.where(owned[:, None], query_grad, 0.0)
    feature_term = (
        feature_term.reshape(t_dev * pixels, chan)
        .at[flat_rows]
        .add(placed)
        .reshape(t_dev, pixels, chan)
    )
    feature_grad = lax.psum_scatter(feature_term, "query", scatter_dimension=1, tiled=True)
    return (query_grad, feature_grad)


def solution(mesh):
    placed = (P("frame", None, None), P(), P(None, "frame", "query"), P("query"), P("query"))
    return jax.shard_map(
        shards,
        mesh=mesh,
        in_specs=placed,
        out_specs=(P("query", None), P("frame", "query", None)),
        check_vma=False,
    )
```

profile of v0, /device:TPU:0, one launch (start us, length us, event | category | flops | bytes accessed | tf_op | source)
XLA Modules:
  0.0 449.0 jit_solution(2033591671652492786)
XLA Ops:
  7.2 0.0 copy-start
  7.2 0.0 all-reduce.7.cloned.1.call-start
  7.2 0.8 compare_and_fusion
  8.1 0.7 broadcast_clamp_fusion
  8.8 0.0 copy-done
  8.8 3.9 gather_fusion
  12.7 1.0 broadcast_select_fusion.3
  13.7 0.0 all-reduce.7.cloned.1.call-update
  13.8 0.0 all-reduce.9.cloned.1.call-start
  13.8 1.7 fusion.43
  15.5 0.7 fusion.42
  16.3 55.2 %all-reduce.7.cloned.1.call-done = bf16[1024,256]{1,0:T(8,128)(2,1)} async-done(((bf16[1024,256]{1,0:T(8,128)(2,1)}), bf16[1024,256]{1,0:T(8,128)(2,1)}) %all-reduce.7.cloned.1.call-update) | async-done | bytes 524304 | tf_op jit(solution)/shard_map/psum | solution.py:24
  71.4 9.1 %fusion.39 = f32[1024,4096]{1,0:T(8,128)} fusion(bf16[1024,256]{1,0:T(8,128)(2,1)} %all-reduce.7.cloned.1.call-done, bf16[1,4096,256]{2,1,0:T(8,128)(2,1)S(1)} %copy-done), kind=kOutput, calls=%fused_computation.66 | convolution fusion | flops 2147483648 | bytes 19398656 | tf_op jit(solution)/shard_map/dot_general | solution.py:35
  80.6 85.7 %fusion.41 = (f32[1024]{0:T(1024)S(1)}, f32[1024,4096]{1,0:T(8,128)}) fusion(f32[]{:T(128)} %bitcast.9, f32[]{:T(128)} %bitcast.8, f32[]{:T(128)} %bitcast.7, f32[]{:T(128)} %bitcast.6, f32[1024,4096]{1,0:T(8,128)} %fusion.39, f32[]{:T(128)} %bitcast.5, f32[]{:T(128)} %bitcast.4, pred[4096]{0:T(1024)(128)(4,1)S(1)} %get-tuple-element.21, f32[]{:T(128)} %bitcast.3, ...), kind=kLoop, calls=%fused_computation.68 | loop fusion | flops 113245184 | bytes 33570852 | tf_op jit(solution)/shard_map/reduce_max | solution.py:43
  166.2 8.1 %fusion.22 = f32[1024]{0:T(1024)S(1)} fusion(f32[1024,4096]{1,0:T(8,128)} %get-tuple-element.5, f32[1024]{0:T(1024)S(1)} %get-tuple-element.4), kind=kLoop, calls=%fused_computation.36 | loop fusion | flops 8387584 | bytes 16785408 | tf_op jit(solution)/shard_map/reduce_sum | solution.py:45
  174.3 8.8 %multiply_reduce_fusion = f32[1024]{0:T(1024)S(1)} fusion(f32[4096]{0:T(1024)S(1)} %get-tuple-element.24, f32[1024]{0:T(1024)S(1)} %bitcast.25, f32[4096]{0:T(1024)S(1)} %get-tuple-element.23, f32[1024]{0:T(1024)S(1)} %bitcast.23, f32[1024]{0:T(1024)S(1)} %fusion.22, f32[1024,4096]{1,0:T(8,128)} %get-tuple-element.5, f32[1024]{0:T(1024)S(1)} %get-tuple-element.4), kind=kLoop, calls=%fused_computation.20 | loop fusion | flops 29359104 | bytes 16830464 | tf_op jit(solution)/shard_map/reduce_sum | solution.py:47
  183.1 15.2 %broadcast_select_fusion.1 = (f32[1024,4096]{1,0:T(8,128)}, f32[1024,4096]{1,0:T(8,128)S(1)}) fusion(pred[4096]{0:T(1024)(128)(4,1)S(1)} %fusion.34, f32[1024]{0:T(1024)S(1)} %multiply_reduce_fusion, f32[4096]{0:T(1024)S(1)} %get-tuple-element.24, f32[1024]{0:T(1024)S(1)} %bitcast.26, f32[4096]{0:T(1024)S(1)} %get-tuple-element.23, f32[1024]{0:T(1024)S(1)} %bitcast.24, ...), kind=kLoop, calls=%fused_computation.38 | loop fusion | flops 33554432 | bytes 50388992 | tf_op jit(solution)/shard_map/jit(_where)/select_n | solution.py:52
  198.3 11.7 %broadcast_select_fusion = (f32[1024,4096]{1,0:T(8,128)}, f32[1024,4096]{1,0:T(8,128)}) fusion(f32[1024,4096]{1,0:T(8,128)S(1)} %get-tuple-element.3, pred[4096]{0:T(1024)(128)(4,1)S(1)} %get-tuple-element.21, pred[4096]{0:T(1024)(128)(4,1)S(1)} %get-tuple-element.22), kind=kLoop, calls=%fused_computation.37 | loop fusion | flops 8388608 | bytes 50339840 | tf_op jit(solution)/shard_map/jit(_where)/select_n | solution.py:52
  210.0 0.0 copy-start.2
  210.0 79.9 %fusion.9 = bf16[1024,4096]{1,0:T(8,128)(2,1)S(1)} fusion(f32[1024,4096]{1,0:T(8,128)} %get-tuple-element.9, f32[1024,4096]{1,0:T(8,128)} %get-tuple-element.8, f32[1024,4096]{1,0:T(8,128)} %get-tuple-element.2, f32[]{:T(128)} %bitcast.9, f32[]{:T(128)} %bitcast.8, f32[]{:T(128)} %bitcast.7, f32[]{:T(128)} %bitcast.6, f32[]{:T(128)} %bitcast.5, f32[]{:T(128)} %bitcast.4, ...), kind=kLoop, calls=%fused_computation.13 | loop fusion | flops 75497472 | bytes 58720292 | tf_op jit(solution)/shard_map/convert_element_type | solution.py:54
  290.0 0.0 copy-start.1
  290.0 3.2 copy-done.1
  293.2 3.3 fusion.37
  296.5 0.0 all-reduce.9.cloned.1.call-update
  296.5 0.0 reduce-scatter.2.cloned.1.call-start
  296.6 0.0 copy-done.2
  296.6 7.8 %fusion.44 = f32[4096,256]{1,0:T(8,128)} fusion(bf16[1024,4096]{1,0:T(8,128)(2,1)} %copy-done.1, bf16[1024,256]{1,0:T(8,128)(2,1)S(1)} %copy-done.2), kind=kOutput, calls=%fused_computation.71 | convolution fusion | flops 2147483648 | bytes 13107200 | tf_op jit(solution)/shard_map/dot_general | solution.py:57
  304.4 48.3 %all-reduce.9.cloned.1.call-done = f32[1024,256]{1,0:T(8,128)} async-done(((f32[1024,256]{1,0:T(8,128)}), f32[1024,256]{1,0:T(8,128)}) %all-reduce.9.cloned.1.call-update) | async-done | bytes 1048592 | tf_op jit(solution)/shard_map/psum | solution.py:60
  352.7 11.2 %scatter_custom_fusion = f32[4096,256]{1,0:T(8,128)} fusion(f32[4096,256]{1,0:T(8,128)} %fusion.44, s32[1024]{0:T(1024)S(1)} %get-tuple-element.7, f32[1024,256]{1,0:T(8,128)} %all-reduce.9.cloned.1.call-done, f32[]{:T(128)} %constant.51.clone.1, pred[1024]{0:T(1024)(128)(4,1)S(1)} %compare_and_fusion), kind=kCustom, calls=%fused_computation.40 | custom fusion | flops 524288 | bytes 5244416 | tf_op jit(solution)/shard_map/scatter-add | solution.py:65
  363.9 0.0 reduce-scatter.2.cloned.1.call-update
  364.0 76.2 %reduce-scatter.2.cloned.1.call-done = f32[1,1024,256]{2,1,0:T(8,128)} async-done(((f32[1,4096,256]{2,1,0:T(8,128)}), f32[1,1024,256]{2,1,0:T(8,128)}) %reduce-scatter.2.cloned.1.call-update) | async-done | bytes 1048592 | tf_op jit(solution)/shard_map/reduce_scatter | solution.py:68
  440.2 2.3 copy.10
  (3 shorter events, 0.0 us)
Async XLA Ops:
  7.2 1.6 copy-start
  7.2 64.2 %all-reduce.7.cloned.1.call-start = ((), (), s32[]{:S(2)}) async-start(), calls=%async_computation.1 | async-start | bytes 1048576 | tf_op jit(solution)/shard_map/psum | solution.py:24
  13.8 338.9 %all-reduce.9.cloned.1.call-start = ((), (), s32[]{:S(2)}) async-start(), calls=%async_computation.2 | async-start | bytes 2097152 | tf_op jit(solution)/shard_map/psum | solution.py:60
  210.0 86.6 %copy-start.2 = (bf16[1024,256]{1,0:T(8,128)(2,1)S(1)}, bf16[1024,256]{1,0:T(8,128)(2,1)}, u32[]{:S(2)}) copy-start(bf16[1024,256]{1,0:T(8,128)(2,1)} %all-reduce.7.cloned.1.call-done) | copy-start | bytes 1572868
  290.0 3.2 copy-start.1
  296.5 143.6 %reduce-scatter.2.cloned.1.call-start = ((), (), s32[]{:S(2)}) async-start(), calls=%async_computation.3 | async-start | bytes 5242880 | tf_op jit(solution)/shard_map/reduce_scatter | solution.py:68
Sparse Core Ops, SparseCore 0:
  13.9 57.4 all-reduce.6
  296.7 55.9 all-reduce.8
  364.1 76.0 reduce-scatter.1
where the time goes:
time: 450 us; the launch traced here: 449 us
  other arithmetic  223 us (50%)
  waiting for transfers between devices  180 us (40%)
  matrix products  20.3 us (5%)
  between operations  13.8 us (3%)
  local copies, waits for them, and re-layouts  11.8 us (3%)
    reduce_max x1, other arithmetic, shards(): top = jnp.max(logits, axis=1, keepdims=True)  85.7 us
    convert_element_type x1, other arithmetic, shards(): dcost = dcost.astype(jnp.bfloat16)  79.9 us
    reduce_scatter x1, waiting for transfers between devices, shards(): lax.psum_scatter(feature_term, 'query', scatter_dimension=1, tiled=True)  76.2 us
    psum x1, waiting for transfers between devices, shards(): qfeat = lax.psum(picked.astype(jnp.bfloat16), 'frame')  55.2 us
    psum x1, waiting for transfers between devices, shards(): query_grad = lax.psum(query_part, 'frame')  48.3 us
    select_n x2, other arithmetic, shards(): masked = jnp.where(col_masks[b], dlogit, 0.0)  26.9 us
    scatter-add x1, other arithmetic, shards(): feature_term = feature_term.reshape(t_dev * pixels, chan).at[flat_rows].a...  11.2 us
    dot_general x1, matrix products, shards(): lax.dot_general(qfeat, frame_map, (((1,), (1,)), ((), ())), preferred_ele...  9.14 us
  transfers between devices with their start and end apart: 3, of which 3 were waited for; matrix products, arithmetic and copies ran while one was open for 2% of the time, Pallas kernels for 0%

commit v1 on v0

--- a/solution.py
+++ b/solution.py
@@ -21,7 +21,7 @@
     flat_rows = jnp.clip(local_frame, 0, t_dev - 1) * pixels + query_pixel
     flat_maps = features.reshape(t_dev * pixels, chan)
     picked = jnp.where(owned[:, None], flat_maps[flat_rows], 0).astype(jnp.float32)
-    qfeat = lax.psum(picked.astype(jnp.bfloat16), "frame")
+    qfeat = jnp.sum(lax.all_gather(picked.astype(jnp.bfloat16), "frame"), axis=0)
     where_pix = lax.iota(jnp.int32, pixels)
     column = where_pix % W
     row_pos = (where_pix // W).astype(jnp.float32) - (height - 1) / 2.0

time: 450 us -> 434 us (0.964)
  waiting for transfers between devices: 180 us -> 162 us
    psum x1 -> x0, waiting for transfers between devices: 55.2 us -> none  [shards(): qfeat = lax.psum(picked.astype(jnp.bfloat16), 'frame')]
    all_gather x0 -> x1, waiting for transfers between devices: none -> 37 us  [shards(): lax.all_gather(picked.astype(jnp.bfloat16), 'frame')]
where the time goes in v1:
time: 434 us; the launch traced here: 433 us
  other arithmetic  226 us (52%)
  waiting for transfers between devices  162 us (37%)
  matrix products  19.2 us (4%)
  between operations  13.8 us (3%)
  local copies, waits for them, and re-layouts  11.8 us (3%)
    reduce_max x1, other arithmetic, shards(): top = jnp.max(logits, axis=1, keepdims=True)  85.4 us
    convert_element_type x1, other arithmetic, shards(): dcost = dcost.astype(jnp.bfloat16)  79.6 us
    reduce_scatter x1, waiting for transfers between devices, shards(): lax.psum_scatter(feature_term, 'query', scatter_dimension=1, tiled=True)  76.2 us
    psum x1, waiting for transfers between devices, shards(): query_grad = lax.psum(query_part, 'frame')  49 us
    all_gather x1, waiting for transfers between devices, shards(): lax.all_gather(picked.astype(jnp.bfloat16), 'frame')  37 us
    select_n x2, other arithmetic, shards(): masked = jnp.where(col_masks[b], dlogit, 0.0)  26.9 us
    scatter-add x1, other arithmetic, shards(): feature_term = feature_term.reshape(t_dev * pixels, chan).at[flat_rows].a...  11.2 us
    reduce_sum x1, other arithmetic, shards(): mean_pull = jnp.sum(prob * pull, axis=1, keepdims=True)  8.81 us
  transfers between devices with their start and end apart: 3, of which 3 were waited for; matrix products, arithmetic and copies ran while one was open for 2% of the time, Pallas kernels for 0%

profile of v1, /device:TPU:0, one launch (start us, length us, event | category | flops | bytes accessed | tf_op | source)
XLA Modules:
  0.0 432.9 jit_solution(9875729662502992714)
XLA Ops:
  7.2 0.0 copy-start
  7.2 0.0 all-gather.2.cloned.1.call-start
  7.2 0.8 compare_and_fusion
  8.1 0.7 broadcast_clamp_fusion
  8.8 0.0 copy-done
  8.8 3.9 gather_fusion
  12.7 1.0 bitcast_select_fusion
  13.7 0.0 all-gather.2.cloned.1.call-update
  13.8 0.0 all-reduce.6.cloned.1.call-start
  13.8 1.7 fusion.43
  15.5 0.7 fusion.42
  16.2 37.0 %all-gather.2.cloned.1.call-done = bf16[8,1024,256]{2,1,0:T(8,128)(2,1)} async-done(((bf16[1,1024,256]{2,1,0:T(8,128)(2,1)}), bf16[8,1024,256]{2,1,0:T(8,128)(2,1)}) %all-gather.2.cloned.1.call-update) | async-done | bytes 4194320 | tf_op jit(solution)/shard_map/all_gather | solution.py:24
  53.2 3.0 reduce_sum.30
  56.3 8.1 %fusion.39 = f32[1024,4096]{1,0:T(8,128)} fusion(bf16[1024,256]{1,0:T(8,128)(2,1)S(1)} %reduce_sum.30, bf16[1,4096,256]{2,1,0:T(8,128)(2,1)S(1)} %copy-done), kind=kOutput, calls=%fused_computation.66 | convolution fusion | flops 2147483648 | bytes 19398656 | tf_op jit(solution)/shard_map/dot_general | solution.py:35
  64.4 85.4 %fusion.41 = (f32[1024]{0:T(1024)S(1)}, f32[1024,4096]{1,0:T(8,128)}) fusion(f32[]{:T(128)} %bitcast.10, f32[]{:T(128)} %bitcast.9, f32[]{:T(128)} %bitcast.8, f32[]{:T(128)} %bitcast.7, f32[1024,4096]{1,0:T(8,128)} %fusion.39, f32[]{:T(128)} %bitcast.6, f32[]{:T(128)} %bitcast.5, pred[4096]{0:T(1024)(128)(4,1)S(1)} %get-tuple-element.21, f32[]{:T(128)} %bitcast.4, ...), kind=kLoop, calls=%fused_computation.68 | loop fusion | flops 113245184 | bytes 33570852 | tf_op jit(solution)/shard_map/reduce_max | solution.py:43
  149.8 8.1 %fusion.22 = f32[1024]{0:T(1024)S(1)} fusion(f32[1024,4096]{1,0:T(8,128)} %get-tuple-element.5, f32[1024]{0:T(1024)S(1)} %get-tuple-element.4), kind=kLoop, calls=%fused_computation.36 | loop fusion | flops 8387584 | bytes 16785408 | tf_op jit(solution)/shard_map/reduce_sum | solution.py:45
  157.9 8.8 %multiply_reduce_fusion = f32[1024]{0:T(1024)S(1)} fusion(f32[4096]{0:T(1024)S(1)} %get-tuple-element.24, f32[1024]{0:T(1024)S(1)} %bitcast.27, f32[4096]{0:T(1024)S(1)} %get-tuple-element.23, f32[1024]{0:T(1024)S(1)} %bitcast.25, f32[1024]{0:T(1024)S(1)} %fusion.22, f32[1024,4096]{1,0:T(8,128)} %get-tuple-element.5, f32[1024]{0:T(1024)S(1)} %get-tuple-element.4), kind=kLoop, calls=%fused_computation.20 | loop fusion | flops 29359104 | bytes 16830464 | tf_op jit(solution)/shard_map/reduce_sum | solution.py:47
  166.7 15.2 %broadcast_select_fusion.1 = (f32[1024,4096]{1,0:T(8,128)}, f32[1024,4096]{1,0:T(8,128)S(1)}) fusion(pred[4096]{0:T(1024)(128)(4,1)S(1)} %fusion.34, f32[1024]{0:T(1024)S(1)} %multiply_reduce_fusion, f32[4096]{0:T(1024)S(1)} %get-tuple-element.24, f32[1024]{0:T(1024)S(1)} %bitcast.28, f32[4096]{0:T(1024)S(1)} %get-tuple-element.23, f32[1024]{0:T(1024)S(1)} %bitcast.26, ...), kind=kLoop, calls=%fused_computation.38 | loop fusion | flops 33554432 | bytes 50388992 | tf_op jit(solution)/shard_map/jit(_where)/select_n | solution.py:52
  181.9 11.7 %broadcast_select_fusion = (f32[1024,4096]{1,0:T(8,128)}, f32[1024,4096]{1,0:T(8,128)}) fusion(f32[1024,4096]{1,0:T(8,128)S(1)} %get-tuple-element.3, pred[4096]{0:T(1024)(128)(4,1)S(1)} %get-tuple-element.21, pred[4096]{0:T(1024)(128)(4,1)S(1)} %get-tuple-element.22), kind=kLoop, calls=%fused_computation.37 | loop fusion | flops 8388608 | bytes 50339840 | tf_op jit(solution)/shard_map/jit(_where)/select_n | solution.py:52
  193.6 79.6 %fusion.9 = bf16[1024,4096]{1,0:T(8,128)(2,1)S(1)} fusion(f32[1024,4096]{1,0:T(8,128)} %get-tuple-element.9, f32[1024,4096]{1,0:T(8,128)} %get-tuple-element.8, f32[1024,4096]{1,0:T(8,128)} %get-tuple-element.2, f32[]{:T(128)} %bitcast.10, f32[]{:T(128)} %bitcast.9, f32[]{:T(128)} %bitcast.8, f32[]{:T(128)} %bitcast.7, f32[]{:T(128)} %bitcast.6, f32[]{:T(128)} %bitcast.5, ...), kind=kLoop, calls=%fused_computation.13 | loop fusion | flops 75497472 | bytes 58720292 | tf_op jit(solution)/shard_map/convert_element_type | solution.py:54
  273.3 0.0 copy-start.1
  273.3 3.2 copy-done.1
  276.5 3.3 fusion.37
  279.8 0.0 all-reduce.6.cloned.1.call-update
  279.8 0.0 reduce-scatter.2.cloned.1.call-start
  279.9 7.8 %fusion.44 = f32[4096,256]{1,0:T(8,128)} fusion(bf16[1024,4096]{1,0:T(8,128)(2,1)} %copy-done.1, bf16[1024,256]{1,0:T(8,128)(2,1)S(1)} %reduce_sum.30), kind=kOutput, calls=%fused_computation.71 | convolution fusion | flops 2147483648 | bytes 13107200 | tf_op jit(solution)/shard_map/dot_general | solution.py:57
  287.7 49.0 %all-reduce.6.cloned.1.call-done = f32[1024,256]{1,0:T(8,128)} async-done(((f32[1024,256]{1,0:T(8,128)}), f32[1024,256]{1,0:T(8,128)}) %all-reduce.6.cloned.1.call-update) | async-done | bytes 1048592 | tf_op jit(solution)/shard_map/psum | solution.py:60
  336.7 11.2 %scatter_custom_fusion = f32[4096,256]{1,0:T(8,128)} fusion(f32[4096,256]{1,0:T(8,128)} %fusion.44, s32[1024]{0:T(1024)S(1)} %get-tuple-element.7, f32[1024,256]{1,0:T(8,128)} %all-reduce.6.cloned.1.call-done, f32[]{:T(128)} %constant.52.clone.1, pred[1024]{0:T(1024)(128)(4,1)S(1)} %compare_and_fusion), kind=kCustom, calls=%fused_computation.40 | custom fusion | flops 524288 | bytes 5244416 | tf_op jit(solution)/shard_map/scatter-add | solution.py:65
  347.9 0.0 reduce-scatter.2.cloned.1.call-update
  347.9 76.2 %reduce-scatter.2.cloned.1.call-done = f32[1,1024,256]{2,1,0:T(8,128)} async-done(((f32[1,4096,256]{2,1,0:T(8,128)}), f32[1,1024,256]{2,1,0:T(8,128)}) %reduce-scatter.2.cloned.1.call-update) | async-done | bytes 1048592 | tf_op jit(solution)/shard_map/reduce_scatter | solution.py:68
  424.1 2.3 copy.9
  (3 shorter events, 0.0 us)
Async XLA Ops:
  7.2 1.6 copy-start
  7.2 46.0 %all-gather.2.cloned.1.call-start = ((), (), s32[]{:S(2)}) async-start(), calls=%async_computation.1 | async-start | bytes 4718592 | tf_op jit(solution)/shard_map/all_gather | solution.py:24
  13.8 322.9 %all-reduce.6.cloned.1.call-start = ((), (), s32[]{:S(2)}) async-start(), calls=%async_computation.2 | async-start | bytes 2097152 | tf_op jit(solution)/shard_map/psum | solution.py:60
  273.3 3.2 copy-start.1
  279.8 144.3 %reduce-scatter.2.cloned.1.call-start = ((), (), s32[]{:S(2)}) async-start(), calls=%async_computation.3 | async-start | bytes 5242880 | tf_op jit(solution)/shard_map/reduce_scatter | solution.py:68
Sparse Core Ops, SparseCore 0:
  13.9 39.2 all-gather.1
  279.9 56.6 all-reduce.5
  348.0 76.0 reduce-scatter.1
